TPU v7x, 32 devices: a whole 2x2x4 slice. The times are simulated.
32 devices in a mesh: depth: 2 (over y), row: 4 (over z), col: 4 (over x, core).
Axes of the slice: x: 2, y: 2, z: 4, core: 2. Of those that a mesh axis runs over, the one named last changes fastest.
Arguments:
- prop: bfloat16 [2, 2, 8192, 8192], P('depth', None, 'row', 'col'), may hold values from -0.046875 to 0.046875
- source: float32 [8192, 256], P(('row', 'col')), may hold values from -6 to 6
- down_init: float32 [2, 8192, 256], P('depth', ('row', 'col')), may hold values from -6 to 6
- up_init: float32 [2, 8192, 256], P('depth', ('row', 'col')), may hold values from -6 to 6
- refl_down: float32 [2, 8192], P('depth', ('row', 'col')), may hold values from -0.6 to 0.6
- refl_up: float32 [2, 8192], P('depth', ('row', 'col')), may hold values from -0.6 to 0.6
Outputs:
- down_field: float32 [2, 8192, 256], P('depth', ('row', 'col'))
- up_field: float32 [2, 8192, 256], P('depth', ('row', 'col'))
All inputs are finite; a program needn't handle non-finite values.
Results may differ from a plain program's by a relative error of at most 0.0041.
Values may be sent and summed in bfloat16 or wider, within the bound.
No kernel may reach another device: no remote copies, remote signals or barrier semaphores. Data moves between devices by JAX's collectives and lax.ppermute only.
A program may use at most 64 MiB of HBM per device.

v0:
```python
import jax
import jax.numpy as jnp
from jax import lax
from jax.sharding import PartitionSpec as P

PASSES = 2


def passed_along(x, axis, by):
    peers = lax.axis_size(axis)
    pairs = [(i, i + by) for i in range(peers) if 0 <= i + by < peers]
    return lax.ppermute(x, axis, pairs)


def complex_join(first, second, sources):
    real_part = first[:, :sources] - second[:, sources:]
    imag_part = first[:, sources:] + second[:, :sources]
    return jnp.concatenate([real_part, imag_part], axis=1)


def downward(weight_real, weight_imag, down_low, sources):
    gathered = lax.all_gather(down_low, "row", axis=0, tiled=True)
    return lax.psum_scatter(
        complex_join(
            jnp.dot(weight_real, gathered, preferred_element_type=jnp.float32),
            jnp.dot(weight_imag, gathered, preferred_element_type=jnp.float32),
            sources,
        ),
        "col",
        scatter_dimension=0,
        tiled=True,
    )


def upward(weight_real, weight_imag, up_low, sources):
    gathered = lax.all_gather(up_low, "col", axis=0, tiled=True)
    numbers = (((0,), (0,)), ((), ()))
    first = lax.dot_general(weight_real, gathered, numbers, preferred_element_type=jnp.float32)
    second = lax.dot_general(weight_imag, gathered, numbers, preferred_element_type=jnp.float32)
    return lax.psum_scatter(
        complex_join(first, second, sources), "row", scatter_dimension=0, tiled=True
    )


def send_trans(trans):
    return passed_along(trans, "depth", 1)


def send_back(back):
    return passed_along(back, "depth", -1)


def body(prop, source, down_init, up_init, refl_down, refl_up):
    weight_real = prop[0, 0]
    weight_imag = prop[0, 1]
    sources = down_init.shape[2] // 2
    at_surface = lax.axis_index("depth") == 0
    refl_above = refl_down[0][:, None]
    refl_below = refl_up[0][:, None]
    down = down_init[0]
    up = up_init[0]
    for sweep in range(PASSES):
        down_low = down.astype(jnp.bfloat16)
        up_low = up.astype(jnp.bfloat16)
        trans = downward(weight_real, weight_imag, down_low, sources)
        from_above = send_trans(trans)
        back = upward(weight_real, weight_imag, up_low, sources)
        from_below = send_back(back)
        above = jnp.where(at_surface, source, from_above)
        down = above + refl_above * back
        up = from_below + refl_below * trans
    return (down[None], up[None])


def solution(mesh):
    placed = (
        P("depth", None, "row", "col"),
        P(("row", "col"), None),
        P("depth", ("row", "col"), None),
        P("depth", ("row", "col"), None),
        P("depth", ("row", "col")),
        P("depth", ("row", "col")),
    )
    return jax.shard_map(
        body,
        mesh=mesh,
        in_specs=placed,
        out_specs=(P("depth", ("row", "col"), None), P("depth", ("row", "col"), None)),
        check_vma=False,
    )
```

profile of v0, /device:TPU:0, one launch (start us, length us, event | category | flops | bytes accessed | tf_op | source)
XLA Modules:
  0.0 290.8 jit_solution(9658612321237586070)
XLA Ops:
  7.2 1.8 convert_element_type.18
  9.1 1.8 convert_element_type.20
  10.9 29.9 %all-gather.11.cloned.1.call-done = bf16[1,2048,256]{2,1,0:T(8,128)(2,1)} async-done(((bf16[1,512,256]{2,1,0:T(8,128)(2,1)}), bf16[1,2048,256]{2,1,0:T(8,128)(2,1)}) %all-gather.11.cloned.1.call-update) | async-done | bytes 1048592 | tf_op jit(solution)/shard_map/all_gather | solution.py:22
  40.8 6.1 %fusion.6 = f32[2048,256]{0,1:T(8,128)S(1)} fusion(bf16[1,2,2048,2048]{3,2,1,0:T(8,128)(2,1)} %param.6, bf16[1,2048,256]{2,1,0:T(8,128)(2,1)} %all-gather.11.cloned.1.call-done), kind=kOutput, calls=%fused_computation.6 | convolution fusion | flops 2147483648 | bytes 11534336 | tf_op jit(solution)/shard_map/dot_general | solution.py:26
  47.0 2.4 copy-done.6
  49.6 2.4 fusion.14
  52.3 1.5 pad_maximum_fusion
  53.9 5.3 %all-gather.13.cloned.1.call-done = bf16[1,2048,256]{2,1,0:T(8,128)(2,1)} async-done(((bf16[1,512,256]{2,1,0:T(8,128)(2,1)}), bf16[1,2048,256]{2,1,0:T(8,128)(2,1)}) %all-gather.13.cloned.1.call-update) | async-done | bytes 1048592 | tf_op jit(solution)/shard_map/all_gather | solution.py:36
  59.2 6.1 %fusion.4 = f32[2048,256]{0,1:T(8,128)S(1)} fusion(bf16[1,2,2048,2048]{3,2,1,0:T(8,128)(2,1)} %param.6, bf16[1,2048,256]{2,1,0:T(8,128)(2,1)} %all-gather.13.cloned.1.call-done), kind=kOutput, calls=%fused_computation.4 | convolution fusion | flops 2147483648 | bytes 11534336 | tf_op jit(solution)/shard_map/dot_general | solution.py:39
  65.3 6.1 %fusion.12 = f32[2048,256]{0,1:T(8,128)S(1)} fusion(bf16[1,2,2048,2048]{3,2,1,0:T(8,128)(2,1)} %param.6, bf16[1,2048,256]{2,1,0:T(8,128)(2,1)S(1)} %copy-done.7), kind=kOutput, calls=%fused_computation.12 | convolution fusion | flops 2147483648 | bytes 11534336 | tf_op jit(solution)/shard_map/dot_general | solution.py:38
  71.7 1.5 pad_maximum_fusion.1
  73.2 20.0 %reduce-scatter.5.cloned.1.call-done = f32[512,256]{0,1:T(8,128)} async-done(((f32[2048,256]{0,1:T(8,128)}), f32[512,256]{0,1:T(8,128)}) %reduce-scatter.5.cloned.1.call-update) | async-done | bytes 524304 | tf_op jit(solution)/shard_map/reduce_scatter | solution.py:23
  93.2 3.5 %collective-permute-start = (f32[512,256]{0,1:T(8,128)}, f32[512,256]{0,1:T(8,128)S(1)}, u32[]{:S(2)}, u32[]{:S(2)}) collective-permute-start(f32[512,256]{0,1:T(8,128)} %reduce-scatter.5.cloned.1.call-done), channel_id=1, source_target_pairs={{0,16},{1,17},{2,18},{3,19},{4,20},{5,21},{6,22},{7,23},{8,24},{9,... | collective-permute-start | bytes 1572872 | tf_op jit(solution)/shard_map/ppermute | solution.py:12
  96.9 42.4 %reduce-scatter.7.cloned.1.call-done = f32[512,256]{0,1:T(8,128)} async-done(((f32[2048,256]{0,1:T(8,128)}), f32[512,256]{0,1:T(8,128)}) %reduce-scatter.7.cloned.1.call-update) | async-done | bytes 524304 | tf_op jit(solution)/shard_map/reduce_scatter | solution.py:40
  139.3 2.0 add_convert_fusion.1
  141.4 1.3 collective-permute-start.2
  142.7 14.1 %collective-permute-done.2 = f32[512,256]{0,1:T(8,128)S(1)} collective-permute-done((f32[512,256]{0,1:T(8,128)S(1)}, f32[512,256]{0,1:T(8,128)S(1)}, u32[]{:S(2)}, u32[]{:S(2)}) %collective-permute-start.2) | collective-permute-done | bytes 524320 | tf_op jit(solution)/shard_map/ppermute | solution.py:12
  157.9 10.9 %all-gather.7.cloned.1.call-done = bf16[2048,256]{0,1:T(8,128)(2,1)} async-done(((bf16[512,256]{0,1:T(8,128)(2,1)}), bf16[2048,256]{0,1:T(8,128)(2,1)}) %all-gather.7.cloned.1.call-update) | async-done | bytes 1048592 | tf_op jit(solution)/shard_map/all_gather | solution.py:22
  168.8 6.1 %fusion.30 = f32[2048,256]{0,1:T(8,128)S(1)} fusion(bf16[2048,256]{0,1:T(8,128)(2,1)} %all-gather.7.cloned.1.call-done, bf16[1,2,2048,2048]{3,2,1,0:T(8,128)(2,1)} %param.6), kind=kOutput, calls=%fused_computation.26 | convolution fusion | flops 2147483648 | bytes 11534336 | tf_op jit(solution)/shard_map/dot_general | solution.py:26
  174.9 6.1 %fusion.24 = f32[2048,256]{0,1:T(8,128)S(1)} fusion(bf16[2048,256]{0,1:T(8,128)(2,1)S(1)} %copy-done.9, bf16[1,2,2048,2048]{3,2,1,0:T(8,128)(2,1)} %param.6), kind=kOutput, calls=%fused_computation.24 | convolution fusion | flops 2147483648 | bytes 11534336 | tf_op jit(solution)/shard_map/dot_general | solution.py:25
  181.3 1.5 pad_maximum_fusion.2
  182.9 4.1 %all-gather.9.cloned.1.call-done = bf16[2048,256]{0,1:T(8,128)(2,1)} async-done(((bf16[512,256]{0,1:T(8,128)(2,1)}), bf16[2048,256]{0,1:T(8,128)(2,1)}) %all-gather.9.cloned.1.call-update) | async-done | bytes 1048592 | tf_op jit(solution)/shard_map/all_gather | solution.py:36
  187.0 6.1 %fusion.33 = f32[2048,256]{0,1:T(8,128)S(1)} fusion(bf16[2048,256]{0,1:T(8,128)(2,1)} %all-gather.9.cloned.1.call-done, bf16[1,2,2048,2048]{3,2,1,0:T(8,128)(2,1)} %param.6), kind=kOutput, calls=%fused_computation.27 | convolution fusion | flops 2147483648 | bytes 11534336 | tf_op jit(solution)/shard_map/dot_general | solution.py:39
  193.1 6.1 %fusion.27 = f32[2048,256]{0,1:T(8,128)S(1)} fusion(bf16[2048,256]{0,1:T(8,128)(2,1)S(1)} %copy-done.8, bf16[1,2,2048,2048]{3,2,1,0:T(8,128)(2,1)} %param.6), kind=kOutput, calls=%fused_computation.25 | convolution fusion | flops 2147483648 | bytes 11534336 | tf_op jit(solution)/shard_map/dot_general | solution.py:38
  199.6 1.5 pad_maximum_fusion.3
  201.1 19.9 %reduce-scatter.9.cloned.1.call-done = f32[512,256]{0,1:T(8,128)} async-done(((f32[2048,256]{0,1:T(8,128)}), f32[512,256]{0,1:T(8,128)}) %reduce-scatter.9.cloned.1.call-update) | async-done | bytes 524304 | tf_op jit(solution)/shard_map/reduce_scatter | solution.py:23
  221.0 3.6 %collective-permute-start.1 = (f32[512,256]{0,1:T(8,128)}, f32[512,256]{0,1:T(8,128)S(1)}, u32[]{:S(2)}, u32[]{:S(2)}) collective-permute-start(f32[512,256]{0,1:T(8,128)} %reduce-scatter.9.cloned.1.call-done), channel_id=1, source_target_pairs={{0,16},{1,17},{2,18},{3,19},{4,20},{5,21},{6,22},{7,23},{8,24},{9,... | collective-permute-start | bytes 1572872 | tf_op jit(solution)/shard_map/ppermute | solution.py:12
  224.6 42.8 %reduce-scatter.11.cloned.1.call-done = f32[512,256]{0,1:T(8,128)} async-done(((f32[2048,256]{0,1:T(8,128)}), f32[512,256]{0,1:T(8,128)}) %reduce-scatter.11.cloned.1.call-update) | async-done | bytes 524304 | tf_op jit(solution)/shard_map/reduce_scatter | solution.py:40
  267.3 1.3 collective-permute-start.3
  268.6 1.2 add_bitcast_fusion.1
  269.8 1.0 copy.10
  270.8 12.1 %collective-permute-done.3 = f32[512,256]{0,1:T(8,128)S(1)} collective-permute-done((f32[512,256]{0,1:T(8,128)}, f32[512,256]{0,1:T(8,128)S(1)}, u32[]{:S(2)}, u32[]{:S(2)}) %collective-permute-start.3) | collective-permute-done | bytes 524320 | tf_op jit(solution)/shard_map/ppermute | solution.py:12
  (47 shorter events, 4.1 us)
Async XLA Ops:
  7.2 33.6 %all-gather.11.cloned.1.call-start = ((), (), s32[]{:S(2)}) async-start(), calls=%async_computation.10 | async-start | bytes 1310720 | tf_op jit(solution)/shard_map/all_gather | solution.py:22
  9.0 50.2 %all-gather.13.cloned.1.call-start = ((), (), s32[]{:S(2)}) async-start(), calls=%async_computation.11 | async-start | bytes 1310720 | tf_op jit(solution)/shard_map/all_gather | solution.py:36
  10.9 82.3 %reduce-scatter.5.cloned.1.call-start = ((), (), s32[]{:S(2)}) async-start(), calls=%async_computation.4 | async-start | bytes 2621440 | tf_op jit(solution)/shard_map/reduce_scatter | solution.py:23
  40.8 8.6 %copy-start.6 = (bf16[1,2,2048,2048]{3,2,1,0:T(8,128)(2,1)S(1)}, bf16[1,2,2048,2048]{3,2,1,0:T(8,128)(2,1)}, u32[]{:S(2)}) copy-start(bf16[1,2,2048,2048]{3,2,1,0:T(8,128)(2,1)} %param.6) | copy-start | bytes 50331652
  40.8 8.8 %copy-start.10 = (bf16[1,2048,256]{2,1,0:T(8,128)(2,1)S(1)}, bf16[1,2048,256]{2,1,0:T(8,128)(2,1)}, u32[]{:S(2)}) copy-start(bf16[1,2048,256]{2,1,0:T(8,128)(2,1)} %all-gather.11.cloned.1.call-done) | copy-start | bytes 3145732
  53.8 85.5 %reduce-scatter.7.cloned.1.call-start = ((), (), s32[]{:S(2)}) async-start(), calls=%async_computation.5 | async-start | bytes 2621440 | tf_op jit(solution)/shard_map/reduce_scatter | solution.py:40
  59.2 6.1 %copy-start.7 = (bf16[1,2048,256]{2,1,0:T(8,128)(2,1)S(1)}, bf16[1,2048,256]{2,1,0:T(8,128)(2,1)}, u32[]{:S(2)}) copy-start(bf16[1,2048,256]{2,1,0:T(8,128)(2,1)} %all-gather.13.cloned.1.call-done) | copy-start | bytes 3145732
  73.1 23.6 %copy-start.2 = (f32[512,256]{1,0:T(8,128)S(1)}, f32[512,256]{1,0:T(8,128)}, u32[]{:S(2)}) copy-start(f32[512,256]{1,0:T(8,128)} %param.7) | copy-start | bytes 1572868
  73.1 66.2 %copy-start.5 = (f32[1,512]{1,0:T(1,128)S(1)}, f32[1,512]{1,0:T(1,128)}, u32[]{:S(2)}) copy-start(f32[1,512]{1,0:T(1,128)} %param.10) | copy-start | bytes 6148
  73.2 83.7 %copy-start.4 = (f32[1,512]{1,0:T(1,128)S(1)}, f32[1,512]{1,0:T(1,128)}, u32[]{:S(2)}) copy-start(f32[1,512]{1,0:T(1,128)} %param.11) | copy-start | bytes 6148
  73.2 95.6 %all-gather.7.cloned.1.call-start = ((), (), s32[]{:S(2)}) async-start(), calls=%async_computation.6 | async-start | bytes 1310720 | tf_op jit(solution)/shard_map/all_gather | solution.py:22
  93.2 63.6 %copy-start = (f32[512,256]{0,1:T(8,128)S(1)}, f32[512,256]{0,1:T(8,128)}, u32[]{:S(2)}) copy-start(f32[512,256]{0,1:T(8,128)} %reduce-scatter.5.cloned.1.call-done) | copy-start | bytes 1572868
  93.2 46.2 %collective-permute-start = (f32[512,256]{0,1:T(8,128)}, f32[512,256]{0,1:T(8,128)S(1)}, u32[]{:S(2)}, u32[]{:S(2)}) collective-permute-start(f32[512,256]{0,1:T(8,128)} %reduce-scatter.5.cloned.1.call-done), channel_id=1, source_target_pairs={{0,16},{1,17},{2,18},{3,19},{4,20},{5,21},{6,22},{7,23},{8,24},{9,... | collective-permute-start | bytes 1572872 | tf_op jit(solution)/shard_map/ppermute | solution.py:12
  139.3 2.1 copy-start.1
  141.3 45.7 %all-gather.9.cloned.1.call-start = ((), (), s32[]{:S(2)}) async-start(), calls=%async_computation.8 | async-start | bytes 1310720 | tf_op jit(solution)/shard_map/all_gather | solution.py:36
  141.4 15.4 %collective-permute-start.2 = (f32[512,256]{0,1:T(8,128)S(1)}, f32[512,256]{0,1:T(8,128)S(1)}, u32[]{:S(2)}, u32[]{:S(2)}) collective-permute-start(f32[512,256]{0,1:T(8,128)S(1)} %copy-done.1), channel_id=1, source_target_pairs={{16,0},{17,1},{18,2},{19,3},{20,4},{21,5},{22,6},{23,7},{24,8},{25... | collective-permute-start | bytes 1572872 | tf_op jit(solution)/shard_map/ppermute | solution.py:12
  157.7 63.3 %reduce-scatter.9.cloned.1.call-start = ((), (), s32[]{:S(2)}) async-start(), calls=%async_computation.7 | async-start | bytes 2621440 | tf_op jit(solution)/shard_map/reduce_scatter | solution.py:23
  168.8 6.2 %copy-start.9 = (bf16[2048,256]{0,1:T(8,128)(2,1)S(1)}, bf16[2048,256]{0,1:T(8,128)(2,1)}, u32[]{:S(2)}) copy-start(bf16[2048,256]{0,1:T(8,128)(2,1)} %all-gather.7.cloned.1.call-done) | copy-start | bytes 3145732
  182.8 84.5 %reduce-scatter.11.cloned.1.call-start = ((), (), s32[]{:S(2)}) async-start(), calls=%async_computation.9 | async-start | bytes 2621440 | tf_op jit(solution)/shard_map/reduce_scatter | solution.py:40
  187.0 6.1 %copy-start.8 = (bf16[2048,256]{0,1:T(8,128)(2,1)S(1)}, bf16[2048,256]{0,1:T(8,128)(2,1)}, u32[]{:S(2)}) copy-start(bf16[2048,256]{0,1:T(8,128)(2,1)} %all-gather.9.cloned.1.call-done) | copy-start | bytes 3145732
  221.0 61.9 %copy-start.3 = (f32[512,256]{0,1:T(8,128)S(1)}, f32[512,256]{0,1:T(8,128)}, u32[]{:S(2)}) copy-start(f32[512,256]{0,1:T(8,128)} %reduce-scatter.9.cloned.1.call-done) | copy-start | bytes 1572868
  221.0 47.6 %collective-permute-start.1 = (f32[512,256]{0,1:T(8,128)}, f32[512,256]{0,1:T(8,128)S(1)}, u32[]{:S(2)}, u32[]{:S(2)}) collective-permute-start(f32[512,256]{0,1:T(8,128)} %reduce-scatter.9.cloned.1.call-done), channel_id=1, source_target_pairs={{0,16},{1,17},{2,18},{3,19},{4,20},{5,21},{6,22},{7,23},{8,24},{9,... | collective-permute-start | bytes 1572872 | tf_op jit(solution)/shard_map/ppermute | solution.py:12
  267.3 15.6 %collective-permute-start.3 = (f32[512,256]{0,1:T(8,128)}, f32[512,256]{0,1:T(8,128)S(1)}, u32[]{:S(2)}, u32[]{:S(2)}) collective-permute-start(f32[512,256]{0,1:T(8,128)} %reduce-scatter.11.cloned.1.call-done), channel_id=1, source_target_pairs={{16,0},{17,1},{18,2},{19,3},{20,4},{21,5},{22,6},{23,7},{24,8},{25... | collective-permute-start | bytes 1572872 | tf_op jit(solution)/shard_map/ppermute | solution.py:12
Sparse Core Ops, SparseCore 0:
  10.1 30.6 all-gather.10
  42.9 16.2 all-gather.12
  61.7 31.4 reduce-scatter.4
  95.4 43.8 reduce-scatter.6
  141.5 27.2 all-gather.6
  170.8 16.2 all-gather.8
  189.5 31.4 reduce-scatter.8
  223.4 43.8 reduce-scatter.10
where the time goes:
time: 291 us
  waiting for transfers between devices  202 us (69%)
  matrix products  45.2 us (16%)
  other arithmetic  14.6 us (5%)
  between operations  14.3 us (5%)
  starting transfers between devices  10.2 us (4%)
  local copies, waits for them, and re-layouts  4.91 us (2%)
    reduce_scatter x2, waiting for transfers between devices, upward(): lax.psum_scatter(complex_join(first, second, sources), 'row', scatter_dim...  85.2 us
    all_gather x2, waiting for transfers between devices, downward(): gathered = lax.all_gather(down_low, 'row', axis=0, tiled=True)  40.8 us
    reduce_scatter x2, waiting for transfers between devices, downward(): lax.psum_scatter(complex_join(jnp.dot(weight_real, gathered, preferred_el...  39.9 us
    ppermute x4, waiting for transfers between devices, passed_along(): return lax.ppermute(x, axis, pairs)  26.2 us
    dot_general x2, matrix products, downward(): jnp.dot(weight_imag, gathered, preferred_element_type=jnp.float32)  12.3 us
    dot_general x2, matrix products, upward(): lax.dot_general(weight_real, gathered, numbers, preferred_element_type=jn...  12.3 us
    dot_general x2, matrix products, upward(): lax.dot_general(weight_imag, gathered, numbers, preferred_element_type=jn...  12.2 us
    ppermute x4, starting transfers between devices, passed_along(): return lax.ppermute(x, axis, pairs)  9.66 us
  transfers between devices with their start and end apart: 12, of which 10 were waited for; matrix products, arithmetic and copies ran while one was open for 20% of the time, Pallas kernels for 0%

commit v1 on v0

--- a/solution.py
+++ b/solution.py
@@ -4,6 +4,19 @@
 from jax.sharding import PartitionSpec as P
 
 PASSES = 2
+
+
+def collect(x, axis, dim):
+    ways = lax.axis_size(axis)
+    up = [(d, (d + 1) % ways) for d in range(ways)]
+    down = [(d, (d - 1) % ways) for d in range(ways)]
+    earlier, later = ([x], [x])
+    for _ in range(ways // 2):
+        earlier.append(lax.ppermute(earlier[-1], axis, up))
+    for _ in range((ways - 1) // 2):
+        later.append(lax.ppermute(later[-1], axis, down))
+    line = jnp.concatenate([*earlier[::-1], *later[1:]], axis=dim)
+    return jnp.roll(line, (lax.axis_index(axis) - ways // 2) * x.shape[dim], axis=dim)
 
 
 def passed_along(x, axis, by):
@@ -33,7 +46,7 @@
 
 
 def upward(weight_real, weight_imag, up_low, sources):
-    gathered = lax.all_gather(up_low, "col", axis=0, tiled=True)
+    gathered = collect(up_low, "col", 0)
     numbers = (((0,), (0,)), ((), ()))
     first = lax.dot_general(weight_real, gathered, numbers, preferred_element_type=jnp.float32)
     second = lax.dot_general(weight_imag, gathered, numbers, preferred_element_type=jnp.float32)

time: 291 us -> 275 us (0.945)
  waiting for transfers between devices: 202 us -> 173 us
  other arithmetic: 14.6 us -> 24.1 us
  starting transfers between devices: 10.2 us -> 16.9 us
    reduce_scatter x2, waiting for transfers between devices: 39.9 us -> 63.9 us  [downward(): lax.psum_scatter(complex_join(jnp.dot(weight_real, gathered, preferred_el...]
    reduce_scatter x2, waiting for transfers between devices: 85.2 us -> 63.1 us  [upward(): lax.psum_scatter(complex_join(first, second, sources), 'row', scatter_dim...]
    all_gather x2, waiting for transfers between devices: 40.8 us -> 20.7 us  [downward(): gathered = lax.all_gather(down_low, 'row', axis=0, tiled=True)]
    ppermute x4, waiting for transfers between devices: 26.2 us -> 12 us  [passed_along(): return lax.ppermute(x, axis, pairs)]
    ppermute x0 -> x6, waiting for transfers between devices: none -> 12.9 us  [the longest x4 12.9 us: collect(): earlier.append(lax.ppermute(earlier[-1], axis, up))]
    concatenate x0 -> x2, other arithmetic: none -> 10.9 us  [collect(): jnp.roll(line, (lax.axis_index(axis) - ways // 2) * x.shape[dim], axis=dim)]
    all_gather x2 -> x0, waiting for transfers between devices: 9.43 us -> none  [upward(): gathered = lax.all_gather(up_low, 'col', axis=0, tiled=True)]
    ppermute x0 -> x6, starting transfers between devices: none -> 6.85 us  [the longest x2 3.76 us: collect(): later.append(lax.ppermute(later[-1], axis, down))]
  transfers between devices with their start and end apart: 12 -> 16, of which waited for: 10 -> 12; matrix products, arithmetic and copies ran while one was open for 20% -> 25% of each run, Pallas kernels for 0% -> 0%
where the time goes in v1:
time: 275 us
  waiting for transfers between devices  173 us (63%)
  matrix products  44.3 us (16%)
  other arithmetic  24.1 us (9%)
  starting transfers between devices  16.9 us (6%)
  between operations  14.4 us (5%)
    reduce_scatter x2, waiting for transfers between devices, downward(): lax.psum_scatter(complex_join(jnp.dot(weight_real, gathered, preferred_el...  63.9 us
    reduce_scatter x2, waiting for transfers between devices, upward(): lax.psum_scatter(complex_join(first, second, sources), 'row', scatter_dim...  63.1 us
    all_gather x2, waiting for transfers between devices, downward(): gathered = lax.all_gather(down_low, 'row', axis=0, tiled=True)  20.7 us
    ppermute x4, waiting for transfers between devices, collect(): earlier.append(lax.ppermute(earlier[-1], axis, up))  12.9 us
    dot_general x2, matrix products, downward(): jnp.dot(weight_real, gathered, preferred_element_type=jnp.float32)  12.3 us
    dot_general x2, matrix products, downward(): jnp.dot(weight_imag, gathered, preferred_element_type=jnp.float32)  12.2 us
    ppermute x4, waiting for transfers between devices, passed_along(): return lax.ppermute(x, axis, pairs)  12 us
    dot_general x2, matrix products, upward(): lax.dot_general(weight_imag, gathered, numbers, preferred_element_type=jn...  11.5 us
  transfers between devices with their start and end apart: 16, of which 12 were waited for; matrix products, arithmetic and copies ran while one was open for 25% of the time, Pallas kernels for 0%

profile of v1, /device:TPU:0, one launch (start us, length us, event | category | flops | bytes accessed | tf_op | source)
XLA Modules:
  0.0 274.7 jit_solution(13636429972145177001)
XLA Ops:
  8.8 2.0 collective-permute-start.3
  10.8 4.1 %collective-permute-done.1 = bf16[512,256]{1,0:T(8,128)(2,1)S(1)} collective-permute-done((bf16[512,256]{1,0:T(8,128)(2,1)S(1)}, bf16[512,256]{1,0:T(8,128)(2,1)S(1)}, u32[]{:S(2)}, u32[]{:S(2)}) %collective-permute-start.1) | collective-permute-done | bytes 262176 | tf_op jit(solution)/shard_map/ppermute | solution.py:15
  14.9 2.5 collective-permute-start.2
  17.4 1.8 convert_element_type.18
  20.7 9.6 %fusion.52 = bf16[2048,256]{1,0:T(8,128)(2,1)S(1)} fusion(s32[]{:T(128)S(6)} %select_n.28, bf16[512,256]{1,0:T(8,128)(2,1)S(1)} %collective-permute-done.2, bf16[512,256]{1,0:T(8,128)(2,1)S(1)} %collective-permute-done.1, bf16[512,256]{1,0:T(8,128)(2,1)S(1)} %convert_bitcast_fusion, bf16[512,256]{1,0:T(8,128)(2,1)S(1)} %collective-permute-done.3), kind=kLoop, calls=%fused_computation.60 | loop fusion | flops 8388608 | bytes 2097156 | tf_op jit(solution)/shard_map/jit(_roll_dynamic)/concatenate | solution.py:19
  30.3 5.7 %fusion.33 = f32[2048,256]{0,1:T(8,128)S(1)} fusion(bf16[2048,256]{1,0:T(8,128)(2,1)S(1)} %fusion.52, bf16[1,2,2048,2048]{3,2,1,0:T(8,128)(2,1)} %param.8), kind=kOutput, calls=%fused_computation.27 | convolution fusion | flops 2147483648 | bytes 11534336 | tf_op jit(solution)/shard_map/dot_general | solution.py:52
  36.1 2.5 fusion.24
  38.9 1.5 pad_maximum_fusion.1
  40.5 8.6 %all-gather.6.cloned.1.call-done = bf16[1,2048,256]{2,1,0:T(8,128)(2,1)} async-done(((bf16[1,512,256]{2,1,0:T(8,128)(2,1)}), bf16[1,2048,256]{2,1,0:T(8,128)(2,1)}) %all-gather.6.cloned.1.call-update) | async-done | bytes 1048592 | tf_op jit(solution)/shard_map/all_gather | solution.py:35
  49.0 6.1 %fusion.6 = f32[2048,256]{0,1:T(8,128)S(1)} fusion(bf16[1,2,2048,2048]{3,2,1,0:T(8,128)(2,1)} %param.8, bf16[1,2048,256]{2,1,0:T(8,128)(2,1)} %all-gather.6.cloned.1.call-done), kind=kOutput, calls=%fused_computation.6 | convolution fusion | flops 2147483648 | bytes 11534336 | tf_op jit(solution)/shard_map/dot_general | solution.py:39
  55.1 6.2 %fusion.14 = f32[2048,256]{0,1:T(8,128)S(1)} fusion(bf16[1,2,2048,2048]{3,2,1,0:T(8,128)(2,1)} %param.8, bf16[1,2048,256]{2,1,0:T(8,128)(2,1)S(1)} %copy-done.6), kind=kOutput, calls=%fused_computation.14 | convolution fusion | flops 2147483648 | bytes 11534336 | tf_op jit(solution)/shard_map/dot_general | solution.py:38
  61.5 1.5 pad_maximum_fusion
  63.1 31.7 %reduce-scatter.7.cloned.1.call-done = f32[512,256]{0,1:T(8,128)} async-done(((f32[2048,256]{0,1:T(8,128)}), f32[512,256]{0,1:T(8,128)}) %reduce-scatter.7.cloned.1.call-update) | async-done | bytes 524304 | tf_op jit(solution)/shard_map/reduce_scatter | solution.py:53
  94.7 1.4 collective-permute-start.5
  96.2 32.0 %reduce-scatter.5.cloned.1.call-done = f32[512,256]{0,1:T(8,128)} async-done(((f32[2048,256]{0,1:T(8,128)}), f32[512,256]{0,1:T(8,128)}) %reduce-scatter.5.cloned.1.call-update) | async-done | bytes 524304 | tf_op jit(solution)/shard_map/reduce_scatter | solution.py:36
  128.2 3.4 %collective-permute-start = (f32[512,256]{0,1:T(8,128)}, f32[512,256]{0,1:T(8,128)S(1)}, u32[]{:S(2)}, u32[]{:S(2)}) collective-permute-start(f32[512,256]{0,1:T(8,128)} %reduce-scatter.5.cloned.1.call-done), channel_id=1, source_target_pairs={{0,16},{1,17},{2,18},{3,19},{4,20},{5,21},{6,22},{7,23},{8,24},{9,... | collective-permute-start | bytes 1572872 | tf_op jit(solution)/shard_map/ppermute | solution.py:25
  133.1 1.8 collective-permute-start.8
  134.8 5.5 %collective-permute-done.6 = bf16[512,256]{0,1:T(8,128)(2,1)S(1)} collective-permute-done((bf16[512,256]{0,1:T(8,128)(2,1)S(1)}, bf16[512,256]{0,1:T(8,128)(2,1)S(1)}, u32[]{:S(2)}, u32[]{:S(2)}) %collective-permute-start.6) | collective-permute-done | bytes 262176 | tf_op jit(solution)/shard_map/ppermute | solution.py:15
  140.3 2.7 collective-permute-done
  144.2 1.9 collective-permute-done.7
  147.4 5.7 %fusion.39 = f32[2048,256]{0,1:T(8,128)S(1)} fusion(bf16[2048,256]{0,1:T(8,128)(2,1)S(1)} %fusion.45, bf16[1,2,2048,2048]{3,2,1,0:T(8,128)(2,1)} %param.8), kind=kOutput, calls=%fused_computation.29 | convolution fusion | flops 2147483648 | bytes 11534336 | tf_op jit(solution)/shard_map/dot_general | solution.py:52
  153.2 5.7 %fusion.30 = f32[2048,256]{0,1:T(8,128)S(1)} fusion(bf16[2048,256]{0,1:T(8,128)(2,1)S(1)} %fusion.45, bf16[1,2,2048,2048]{3,2,1,0:T(8,128)(2,1)} %param.8), kind=kOutput, calls=%fused_computation.26 | convolution fusion | flops 2147483648 | bytes 11534336 | tf_op jit(solution)/shard_map/dot_general | solution.py:51
  159.2 1.5 pad_maximum_fusion.3
  160.8 12.1 %all-gather.4.cloned.1.call-done = bf16[2048,256]{0,1:T(8,128)(2,1)} async-done(((bf16[512,256]{0,1:T(8,128)(2,1)}), bf16[2048,256]{0,1:T(8,128)(2,1)}) %all-gather.4.cloned.1.call-update) | async-done | bytes 1048592 | tf_op jit(solution)/shard_map/all_gather | solution.py:35
  172.9 6.1 %fusion.36 = f32[2048,256]{0,1:T(8,128)S(1)} fusion(bf16[2048,256]{0,1:T(8,128)(2,1)} %all-gather.4.cloned.1.call-done, bf16[1,2,2048,2048]{3,2,1,0:T(8,128)(2,1)} %param.8), kind=kOutput, calls=%fused_computation.28 | convolution fusion | flops 2147483648 | bytes 11534336 | tf_op jit(solution)/shard_map/dot_general | solution.py:39
  179.1 6.1 %fusion.27 = f32[2048,256]{0,1:T(8,128)S(1)} fusion(bf16[2048,256]{0,1:T(8,128)(2,1)S(1)} %copy-done.7, bf16[1,2,2048,2048]{3,2,1,0:T(8,128)(2,1)} %param.8), kind=kOutput, calls=%fused_computation.25 | convolution fusion | flops 2147483648 | bytes 11534336 | tf_op jit(solution)/shard_map/dot_general | solution.py:38
  185.5 1.5 pad_maximum_fusion.2
  187.0 31.5 %reduce-scatter.11.cloned.1.call-done = f32[512,256]{0,1:T(8,128)} async-done(((f32[2048,256]{0,1:T(8,128)}), f32[512,256]{0,1:T(8,128)}) %reduce-scatter.11.cloned.1.call-update) | async-done | bytes 524304 | tf_op jit(solution)/shard_map/reduce_scatter | solution.py:53
  218.5 1.4 collective-permute-start.9
  219.9 31.9 %reduce-scatter.9.cloned.1.call-done = f32[512,256]{0,1:T(8,128)} async-done(((f32[2048,256]{0,1:T(8,128)}), f32[512,256]{0,1:T(8,128)}) %reduce-scatter.9.cloned.1.call-update) | async-done | bytes 524304 | tf_op jit(solution)/shard_map/reduce_scatter | solution.py:36
  251.8 3.4 %collective-permute-start.4 = (f32[512,256]{0,1:T(8,128)}, f32[512,256]{0,1:T(8,128)S(1)}, u32[]{:S(2)}, u32[]{:S(2)}) collective-permute-start(f32[512,256]{0,1:T(8,128)} %reduce-scatter.9.cloned.1.call-done), channel_id=1, source_target_pairs={{0,16},{1,17},{2,18},{3,19},{4,20},{5,21},{6,22},{7,23},{8,24},{9,... | collective-permute-start | bytes 1572872 | tf_op jit(solution)/shard_map/ppermute | solution.py:25
  257.4 9.3 %collective-permute-done.4 = f32[512,256]{0,1:T(8,128)S(1)} collective-permute-done((f32[512,256]{0,1:T(8,128)}, f32[512,256]{0,1:T(8,128)S(1)}, u32[]{:S(2)}, u32[]{:S(2)}) %collective-permute-start.4) | collective-permute-done | bytes 524320 | tf_op jit(solution)/shard_map/ppermute | solution.py:25
  (49 shorter events, 11.6 us)
Async XLA Ops:
  7.2 41.9 %all-gather.6.cloned.1.call-start = ((), (), s32[]{:S(2)}) async-start(), calls=%async_computation.9 | async-start | bytes 1310720 | tf_op jit(solution)/shard_map/all_gather | solution.py:35
  8.3 6.6 %collective-permute-start.1 = (bf16[512,256]{1,0:T(8,128)(2,1)S(1)}, bf16[512,256]{1,0:T(8,128)(2,1)S(1)}, u32[]{:S(2)}, u32[]{:S(2)}) collective-permute-start(bf16[512,256]{1,0:T(8,128)(2,1)S(1)} %convert_bitcast_fusion), channel_id=1, source_target_pairs={{0,1},{1,2},{2,3},{3,0},{4,5},{5,6},{6,7},{7,4},{8,9},{9,10},{10,1... | collective-permute-start | bytes 786440 | tf_op jit(solution)/shard_map/ppermute | solution.py:15
  8.8 10.5 %collective-permute-start.3 = (bf16[512,256]{1,0:T(8,128)(2,1)S(1)}, bf16[512,256]{1,0:T(8,128)(2,1)S(1)}, u32[]{:S(2)}, u32[]{:S(2)}) collective-permute-start(bf16[512,256]{1,0:T(8,128)(2,1)S(1)} %convert_bitcast_fusion), channel_id=1, source_target_pairs={{0,3},{1,0},{2,1},{3,2},{4,7},{5,4},{6,5},{7,6},{8,11},{9,8},{10,9... | collective-permute-start | bytes 786440 | tf_op jit(solution)/shard_map/ppermute | solution.py:17
  14.9 5.8 %collective-permute-start.2 = (bf16[512,256]{1,0:T(8,128)(2,1)S(1)}, bf16[512,256]{1,0:T(8,128)(2,1)S(1)}, u32[]{:S(2)}, u32[]{:S(2)}) collective-permute-start(bf16[512,256]{1,0:T(8,128)(2,1)S(1)} %collective-permute-done.1), channel_id=1, source_target_pairs={{0,1},{1,2},{2,3},{3,0},{4,5},{5,6},{6,7},{7,4},{8,9},{9,10},{10,1... | collective-permute-start | bytes 786440 | tf_op jit(solution)/shard_map/ppermute | solution.py:15
  19.2 75.5 %reduce-scatter.7.cloned.1.call-start = ((), (), s32[]{:S(2)}) async-start(), calls=%async_computation.5 | async-start | bytes 2621440 | tf_op jit(solution)/shard_map/reduce_scatter | solution.py:53
  20.7 15.3 %copy-start.5 = (bf16[1,2,2048,2048]{3,2,1,0:T(8,128)(2,1)S(1)}, bf16[1,2,2048,2048]{3,2,1,0:T(8,128)(2,1)}, u32[]{:S(2)}) copy-start(bf16[1,2,2048,2048]{3,2,1,0:T(8,128)(2,1)} %param.8) | copy-start | bytes 50331652
  40.4 87.7 %reduce-scatter.5.cloned.1.call-start = ((), (), s32[]{:S(2)}) async-start(), calls=%async_computation.4 | async-start | bytes 2621440 | tf_op jit(solution)/shard_map/reduce_scatter | solution.py:36
  49.0 6.1 %copy-start.6 = (bf16[1,2048,256]{2,1,0:T(8,128)(2,1)S(1)}, bf16[1,2048,256]{2,1,0:T(8,128)(2,1)}, u32[]{:S(2)}) copy-start(bf16[1,2048,256]{2,1,0:T(8,128)(2,1)} %all-gather.6.cloned.1.call-done) | copy-start | bytes 3145732
  63.0 68.6 %copy-start.3 = (f32[1,512]{1,0:T(1,128)S(1)}, f32[1,512]{1,0:T(1,128)}, u32[]{:S(2)}) copy-start(f32[1,512]{1,0:T(1,128)} %param.13) | copy-start | bytes 6148
  63.0 69.8 %copy-start.1 = (f32[512,256]{1,0:T(8,128)S(1)}, f32[512,256]{1,0:T(8,128)}, u32[]{:S(2)}) copy-start(f32[512,256]{1,0:T(8,128)} %param.9) | copy-start | bytes 1572868
  63.0 80.0 %copy-start.4 = (f32[1,512]{1,0:T(1,128)S(1)}, f32[1,512]{1,0:T(1,128)}, u32[]{:S(2)}) copy-start(f32[1,512]{1,0:T(1,128)} %param.12) | copy-start | bytes 6148
  63.0 109.9 %all-gather.4.cloned.1.call-start = ((), (), s32[]{:S(2)}) async-start(), calls=%async_computation.6 | async-start | bytes 1310720 | tf_op jit(solution)/shard_map/all_gather | solution.py:35
  94.7 48.3 %copy-start = (f32[512,256]{0,1:T(8,128)S(1)}, f32[512,256]{0,1:T(8,128)}, u32[]{:S(2)}) copy-start(f32[512,256]{0,1:T(8,128)} %reduce-scatter.7.cloned.1.call-done) | copy-start | bytes 1572868
  94.7 36.9 %collective-permute-start.5 = (f32[512,256]{0,1:T(8,128)}, f32[512,256]{0,1:T(8,128)S(1)}, u32[]{:S(2)}, u32[]{:S(2)}) collective-permute-start(f32[512,256]{0,1:T(8,128)} %reduce-scatter.7.cloned.1.call-done), channel_id=1, source_target_pairs={{16,0},{17,1},{18,2},{19,3},{20,4},{21,5},{22,6},{23,7},{24,8},{25... | collective-permute-start | bytes 1572872 | tf_op jit(solution)/shard_map/ppermute | solution.py:25
  128.2 14.9 %collective-permute-start = (f32[512,256]{0,1:T(8,128)}, f32[512,256]{0,1:T(8,128)S(1)}, u32[]{:S(2)}, u32[]{:S(2)}) collective-permute-start(f32[512,256]{0,1:T(8,128)} %reduce-scatter.5.cloned.1.call-done), channel_id=1, source_target_pairs={{0,16},{1,17},{2,18},{3,19},{4,20},{5,21},{6,22},{7,23},{8,24},{9,... | collective-permute-start | bytes 1572872 | tf_op jit(solution)/shard_map/ppermute | solution.py:25
  132.8 7.5 %collective-permute-start.6 = (bf16[512,256]{0,1:T(8,128)(2,1)S(1)}, bf16[512,256]{0,1:T(8,128)(2,1)S(1)}, u32[]{:S(2)}, u32[]{:S(2)}) collective-permute-start(bf16[512,256]{0,1:T(8,128)(2,1)S(1)} %add_convert_fusion), channel_id=1, source_target_pairs={{0,1},{1,2},{2,3},{3,0},{4,5},{5,6},{6,7},{7,4},{8,9},{9,10},{10,1... | collective-permute-start | bytes 786440 | tf_op jit(solution)/shard_map/ppermute | solution.py:15
  133.1 11.2 %collective-permute-start.8 = (bf16[512,256]{0,1:T(8,128)(2,1)S(1)}, bf16[512,256]{0,1:T(8,128)(2,1)S(1)}, u32[]{:S(2)}, u32[]{:S(2)}) collective-permute-start(bf16[512,256]{0,1:T(8,128)(2,1)S(1)} %add_convert_fusion), channel_id=1, source_target_pairs={{0,3},{1,0},{2,1},{3,2},{4,7},{5,4},{6,5},{7,6},{8,11},{9,8},{10,9... | collective-permute-start | bytes 786440 | tf_op jit(solution)/shard_map/ppermute | solution.py:17
  140.3 5.8 %collective-permute-start.7 = (bf16[512,256]{0,1:T(8,128)(2,1)S(1)}, bf16[512,256]{0,1:T(8,128)(2,1)S(1)}, u32[]{:S(2)}, u32[]{:S(2)}) collective-permute-start(bf16[512,256]{0,1:T(8,128)(2,1)S(1)} %collective-permute-done.6), channel_id=1, source_target_pairs={{0,1},{1,2},{2,3},{3,0},{4,5},{5,6},{6,7},{7,4},{8,9},{9,10},{10,1... | collective-permute-start | bytes 786440 | tf_op jit(solution)/shard_map/ppermute | solution.py:15
  144.0 74.5 %reduce-scatter.11.cloned.1.call-start = ((), (), s32[]{:S(2)}) async-start(), calls=%async_computation.8 | async-start | bytes 2621440 | tf_op jit(solution)/shard_map/reduce_scatter | solution.py:53
  160.8 91.0 %reduce-scatter.9.cloned.1.call-start = ((), (), s32[]{:S(2)}) async-start(), calls=%async_computation.7 | async-start | bytes 2621440 | tf_op jit(solution)/shard_map/reduce_scatter | solution.py:36
  172.9 6.2 %copy-start.7 = (bf16[2048,256]{0,1:T(8,128)(2,1)S(1)}, bf16[2048,256]{0,1:T(8,128)(2,1)}, u32[]{:S(2)}) copy-start(bf16[2048,256]{0,1:T(8,128)(2,1)} %all-gather.4.cloned.1.call-done) | copy-start | bytes 3145732
  218.5 48.2 %copy-start.2 = (f32[512,256]{0,1:T(8,128)S(1)}, f32[512,256]{0,1:T(8,128)}, u32[]{:S(2)}) copy-start(f32[512,256]{0,1:T(8,128)} %reduce-scatter.11.cloned.1.call-done) | copy-start | bytes 1572868
  218.5 36.7 %collective-permute-start.9 = (f32[512,256]{0,1:T(8,128)}, f32[512,256]{0,1:T(8,128)S(1)}, u32[]{:S(2)}, u32[]{:S(2)}) collective-permute-start(f32[512,256]{0,1:T(8,128)} %reduce-scatter.11.cloned.1.call-done), channel_id=1, source_target_pairs={{16,0},{17,1},{18,2},{19,3},{20,4},{21,5},{22,6},{23,7},{24,8},{25... | collective-permute-start | bytes 1572872 | tf_op jit(solution)/shard_map/ppermute | solution.py:25
  251.8 14.9 %collective-permute-start.4 = (f32[512,256]{0,1:T(8,128)}, f32[512,256]{0,1:T(8,128)S(1)}, u32[]{:S(2)}, u32[]{:S(2)}) collective-permute-start(f32[512,256]{0,1:T(8,128)} %reduce-scatter.9.cloned.1.call-done), channel_id=1, source_target_pairs={{0,16},{1,17},{2,18},{3,19},{4,20},{5,21},{6,22},{7,23},{8,24},{9,... | collective-permute-start | bytes 1572872 | tf_op jit(solution)/shard_map/ppermute | solution.py:25
Sparse Core Ops, SparseCore 0:
  19.3 29.6 all-gather.5
  51.3 43.3 reduce-scatter.6
  97.4 30.6 reduce-scatter.4
  144.1 28.8 all-gather.3
  175.1 43.3 reduce-scatter.10
  221.0 30.7 reduce-scatter.8
